TPU v7x, 32 devices: a whole 2x2x4 slice. The times are simulated.
32 devices in a mesh: grp: 2 (over y), col: 4 (over z), row: 2 (over x), limb: 2 (over core).
Axes of the slice: x: 2, y: 2, z: 4, core: 2. Of those that a mesh axis runs over, the one named last changes fastest.
Arguments:
- database: bfloat16 [8192, 8192], P(('grp', 'row'), 'col'), parts along dimension 0, may hold values from -128 to 127, as said below
- lwe_matrix: bfloat16 [8192, 2, 512], P('col', 'limb'), may hold values from -0.0008544922 to 0.0008544922
- secret_ct: float32 [2, 2, 2, 512, 4096], P(None, None, 'limb', 'col', 'row'), may hold values from -6 to 6
Outputs:
- encrypted_product: float32 [4, 2, 4096], P('grp', None, 'row'), parts along dimension 0
There are 2 independent parts, one for each index of `grp`. A program takes and returns all parts, laid end to end along the dimension named above; an argument that names none is the same for every part. Nothing has to cross between parts.
Inputs may be any that keep to these rules, and one draw needn't show every extreme that they name: `database`: whole numbers.
All inputs are finite; a program needn't handle non-finite values.
Results may differ from a plain program's by a relative error of at most 0.0003.
Values sent between devices are 32-bit elements; how exact they have to be, the bound alone decides.
A program may use at most 64 MiB of HBM per device.

v0:
```python
import math
import jax
import jax.numpy as jnp
from jax import lax
from jax.sharding import PartitionSpec as P


def exact_dot(left, right):
    return jnp.dot(left, right, precision=lax.Precision.HIGHEST, preferred_element_type=jnp.float32)


def body(database, lwe_matrix, secret_ct):
    row_count = lax.axis_size("row")
    row_rank = lax.axis_index("row")
    row_dev = database.shape[0]
    degree_all = row_dev * row_count
    sub_rows = row_dev // row_count
    a_panel = lwe_matrix[:, 0, :]
    contract_rows = (((0,), (1,)), ((), ()))
    hint_block = lax.psum_scatter(
        lax.dot_general(a_panel, database, contract_rows, preferred_element_type=jnp.float32),
        "col",
        scatter_dimension=0,
        tiled=True,
    )
    freq_low = jnp.arange(row_count, dtype=jnp.int32)
    odd_index = 2 * freq_low + 1
    by_columns = lax.all_to_all(
        hint_block[:, None, :], "row", split_axis=2, concat_axis=1, tiled=True
    )
    phase_index = freq_low[:, None] * odd_index[None, :] % (2 * row_count)
    angle_small = jnp.pi * phase_index.astype(jnp.float32) / row_count
    mixed_real = jnp.einsum(
        "jas,ak->jks", by_columns, jnp.cos(angle_small), precision=lax.Precision.HIGHEST
    )
    mixed_imag = -jnp.einsum(
        "jas,ak->jks", by_columns, jnp.sin(angle_small), precision=lax.Precision.HIGHEST
    )
    local_rows = row_rank * sub_rows + jnp.arange(sub_rows, dtype=jnp.int32)
    twist_index = odd_index[:, None] * local_rows[None, :] % (2 * degree_all)
    twist_angle = jnp.pi * twist_index.astype(jnp.float32) / degree_all
    twist_cos = jnp.cos(twist_angle)
    twist_sin = jnp.sin(twist_angle)
    turned_real = mixed_real * twist_cos + mixed_imag * twist_sin
    turned_imag = mixed_imag * twist_cos - mixed_real * twist_sin
    back_rows = lax.all_to_all(
        jnp.stack([turned_real, turned_imag]), "row", split_axis=2, concat_axis=3, tiled=True
    )
    point_real = back_rows[0, :, 0, :]
    point_imag = back_rows[1, :, 0, :]
    freq_rows = jnp.arange(row_dev, dtype=jnp.int32)
    table_index = freq_rows[:, None] * freq_rows[None, :] % row_dev
    table_angle = 2.0 * jnp.pi * table_index.astype(jnp.float32) / row_dev
    table_cos = jnp.cos(table_angle)
    table_sin = jnp.sin(table_angle)
    scale_factor = 1.0 / math.sqrt(degree_all)
    spec_real = (exact_dot(point_real, table_cos) + exact_dot(point_imag, table_sin)) * scale_factor
    spec_imag = (exact_dot(point_imag, table_cos) - exact_dot(point_real, table_sin)) * scale_factor
    cipher = secret_ct[:, :, 0]
    prod_real = jnp.sum(spec_real * cipher[:, 0] - spec_imag * cipher[:, 1], axis=1)
    prod_imag = jnp.sum(spec_real * cipher[:, 1] + spec_imag * cipher[:, 0], axis=1)
    slot_total = lax.psum(jnp.stack([prod_real, prod_imag], axis=1), ("col", "limb"))
    return slot_total / math.sqrt(2 * lwe_matrix.shape[2])


def solution(mesh):
    placed = (P(("grp", "row"), "col"), P("col", "limb", None), P(None, None, "limb", "col", "row"))
    return jax.shard_map(
        body, mesh=mesh, in_specs=placed, out_specs=P("grp", None, "row"), check_vma=False
    )
```

profile of v0, /device:TPU:0, one launch (start us, length us, event | category | flops | bytes accessed | tf_op | source)
XLA Modules:
  0.0 506.8 jit_solution(10724719638266237290)
XLA Ops:
  6.5 1.6 copy-done
  8.1 9.6 %fusion.28 = f32[512,2048]{1,0:T(8,128)} fusion(bf16[2048,2048]{1,0:T(8,128)(2,1)} %param.3, bf16[2048,1,512]{2,0,1:T(8,128)(2,1)S(1)} %copy-done), kind=kOutput, calls=%fused_computation.22 | convolution fusion | flops 4294967296 | bytes 14680064 | tf_op jit(solution)/shard_map/dot_general | solution.py:21
  17.8 79.7 %reduce-scatter.2.cloned.1.call-done = f32[128,2048]{1,0:T(8,128)} async-done(((f32[512,2048]{1,0:T(8,128)}), f32[128,2048]{1,0:T(8,128)}) %reduce-scatter.2.cloned.1.call-update) | async-done | bytes 1048592 | tf_op jit(solution)/shard_map/reduce_scatter | solution.py:20
  97.4 3.6 copy.12
  101.0 3.6 all-to-all-start
  104.6 0.2 fusion.34
  104.8 13.3 %all-to-all-done = f32[128,1,2048]{0,1,2:T(1,128)S(1)} async-done(((f32[128,1,2048]{0,1,2:T(1,128)}), f32[128,1,2048]{0,1,2:T(1,128)S(1)}, u32[]{:S(2)}, u32[]{:S(2)}) %all-to-all-start) | async-done | bytes 1048608 | tf_op jit(solution)/shard_map/all_to_all | solution.py:28
  118.1 1.0 copy-done.2
  119.1 1.6 copy.19
  120.7 3.9 convolution_negate_fusion
  124.6 4.7 add_bitcast_fusion
  129.4 0.9 pad_maximum_fusion
  130.3 0.7 copy.14
  131.0 26.6 %all_to_all.21 = f32[2,128,2,1024]{3,1,0,2:T(8,128)S(1)} all-to-all(f32[2,128,2,1024]{3,1,0,2:T(8,128)S(1)} %copy.14), channel_id=1, replica_groups=mesh['grp'=2,'col'=4,'row'=2,'limb'=2] {'row'}, dimensions={2} | all-to-all | bytes 4194304 | tf_op jit(solution)/shard_map/all_to_all | solution.py:46
  157.6 1.2 fusion.69
  158.8 2.5 copy.21
  161.3 77.7 %fusion.8 = f32[128,2048]{1,0:T(8,128)} fusion(f32[128,2048]{0,1:T(8,128)} %bitcast.52), kind=kOutput, calls=%fused_computation.11 | convolution fusion | flops 6501171200 | bytes 2097152 | tf_op jit(solution)/shard_map/dot_general | solution.py:9
  239.0 1.3 copy.20
  240.4 77.4 %fusion.10 = f32[128,2048]{1,0:T(8,128)S(1)} fusion(f32[128,2048]{0,1:T(8,128)} %bitcast.55), kind=kOutput, calls=%fused_computation.12 | convolution fusion | flops 6501171200 | bytes 2097152 | tf_op jit(solution)/shard_map/dot_general | solution.py:9
  317.8 76.7 %fusion.22 = f32[128,2048]{1,0:T(8,128)S(1)} fusion(f32[128,2048]{1,0:T(8,128)S(1)} %copy-done.5, f32[128,2048]{0,1:T(8,128)S(1)} %bitcast.56), kind=kOutput, calls=%fused_computation.17 | convolution fusion | flops 6501695488 | bytes 3145728 | tf_op jit(solution)/shard_map/dot_general | solution.py:9
  394.5 76.5 %fusion.25 = f32[128,2048]{1,0:T(8,128)S(1)} fusion(f32[128,2048]{1,0:T(8,128)S(1)} %fusion.10, f32[128,2048]{0,1:T(8,128)S(1)} %bitcast.53), kind=kOutput, calls=%fused_computation.18 | convolution fusion | flops 6501695488 | bytes 3145728 | tf_op jit(solution)/shard_map/dot_general | solution.py:9
  471.1 0.8 subtract_reduce_fusion
  471.9 27.2 %psum.7 = f32[2,2,2048]{2,0,1:T(2,128)S(1)} all-reduce(f32[2,2,2048]{2,0,1:T(2,128)S(1)} %pad_maximum_fusion.1), channel_id=1, replica_groups=mesh['grp'=2,'col'=4,'row'=2,'limb'=2] {'col','limb'}, use_global_device_ids=true, to_apply=%region_3.4 | all-reduce | flops 8192 | bytes 65536 | tf_op jit(solution)/shard_map/psum | solution.py:62
  499.1 0.6 copy.18
  (16 shorter events, 0.1 us)
Async XLA Ops:
  6.5 1.6 copy-start
  6.5 90.9 %reduce-scatter.2.cloned.1.call-start = ((), (), s32[]{:S(2)}) async-start(), calls=%async_computation.3 | async-start | bytes 5242880 | tf_op jit(solution)/shard_map/reduce_scatter | solution.py:20
  101.0 17.1 %all-to-all-start = ((f32[128,1,2048]{0,1,2:T(1,128)}), f32[128,1,2048]{0,1,2:T(1,128)S(1)}, u32[]{:S(2)}, u32[]{:S(2)}) async-start(f32[128,1,2048]{0,1,2:T(1,128)} %copy.12), calls=%async_computation.1 | async-start | bytes 2097152 | tf_op jit(solution)/shard_map/all_to_all | solution.py:28
  118.1 1.0 copy-start.2
  240.4 77.4 %copy-start.4 = (f32[1,128,2,1024]{1,3,2,0:T(8,128)S(1)}, f32[1,128,2,1024]{1,3,2,0:T(8,128)}, u32[]{:S(2)}) copy-start(f32[1,128,2,1024]{1,3,2,0:T(8,128)} %copy.20) | copy-start | bytes 3145732
  240.4 77.4 %copy-start.5 = (f32[128,2048]{1,0:T(8,128)S(1)}, f32[128,2048]{1,0:T(8,128)}, u32[]{:S(2)}) copy-start(f32[128,2048]{1,0:T(8,128)} %fusion.8) | copy-start | bytes 3145732
  317.8 76.8 %copy-start.3 = (f32[1,128,2,1024]{1,3,2,0:T(8,128)S(1)}, f32[1,128,2,1024]{1,3,2,0:T(8,128)}, u32[]{:S(2)}) copy-start(f32[1,128,2,1024]{1,3,2,0:T(8,128)} %copy.21) | copy-start | bytes 3145732
  394.5 76.5 %copy-start.1 = (f32[2,2,1,128,2048]{4,3,2,1,0:T(8,128)S(1)}, f32[2,2,1,128,2048]{4,3,2,1,0:T(8,128)}, u32[]{:S(2)}) copy-start(f32[2,2,1,128,2048]{4,3,2,1,0:T(8,128)} %param.5) | copy-start | bytes 12582916
Sparse Core Ops, SparseCore 0:
  17.9 79.5 reduce-scatter.1
where the time goes:
time: 514 us; the launch traced here: 507 us
  matrix products  327 us (64%)
  waiting for transfers between devices  93 us (18%)
  blocking collectives  53.8 us (10%)
  local copies, waits for them, and re-layouts  14.1 us (3%)
  between operations  13.7 us (3%)
    dot_general x4, matrix products, exact_dot(): jnp.dot(left, right, precision=lax.Precision.HIGHEST, preferred_element_t...  308 us
    reduce_scatter x1, waiting for transfers between devices, body(): lax.psum_scatter(lax.dot_general(a_panel, database, contract_rows, prefer...  79.7 us
    psum x1, blocking collectives, body(): lax.psum(jnp.stack([prod_real, prod_imag], axis=1), ('col', 'limb'))  27.2 us
    all_to_all x1, blocking collectives, body(): lax.all_to_all(jnp.stack([turned_real, turned_imag]), 'row', split_axis=2...  26.6 us
    all_to_all x1, waiting for transfers between devices, body(): lax.all_to_all(hint_block[:, None, :], 'row', split_axis=2, concat_axis=1...  13.3 us
  transfers between devices with their start and end apart: 2, of which 2 were waited for; matrix products, arithmetic and copies ran while one was open for 0% of the time, Pallas kernels for 0%

commit v1 on v0

--- a/solution.py
+++ b/solution.py
@@ -59,7 +59,9 @@
     cipher = secret_ct[:, :, 0]
     prod_real = jnp.sum(spec_real * cipher[:, 0] - spec_imag * cipher[:, 1], axis=1)
     prod_imag = jnp.sum(spec_real * cipher[:, 1] + spec_imag * cipher[:, 0], axis=1)
-    slot_total = lax.psum(jnp.stack([prod_real, prod_imag], axis=1), ("col", "limb"))
+    slot_total = jnp.sum(
+        lax.all_gather(jnp.stack([prod_real, prod_imag], axis=1), ("col", "limb")), axis=0
+    )
     return slot_total / math.sqrt(2 * lwe_matrix.shape[2])
 
 

time: 514 us -> 502 us (0.977)
  blocking collectives: 53.8 us -> 42 us
    psum x1 -> x0, blocking collectives: 27.2 us -> none  [body(): lax.psum(jnp.stack([prod_real, prod_imag], axis=1), ('col', 'limb'))]
    all_gather x0 -> x1, blocking collectives: none -> 15.3 us  [body(): lax.all_gather(jnp.stack([prod_real, prod_imag], axis=1), ('col', 'limb'))]
where the time goes in v1:
time: 502 us; the launch traced here: 495 us
  matrix products  327 us (65%)
  waiting for transfers between devices  93 us (19%)
  blocking collectives  42 us (8%)
  between operations  13.8 us (3%)
  local copies, waits for them, and re-layouts  13.5 us (3%)
    dot_general x4, matrix products, exact_dot(): jnp.dot(left, right, precision=lax.Precision.HIGHEST, preferred_element_t...  308 us
    reduce_scatter x1, waiting for transfers between devices, body(): lax.psum_scatter(lax.dot_general(a_panel, database, contract_rows, prefer...  79.7 us
    all_to_all x1, blocking collectives, body(): lax.all_to_all(jnp.stack([turned_real, turned_imag]), 'row', split_axis=2...  26.6 us
    all_gather x1, blocking collectives, body(): lax.all_gather(jnp.stack([prod_real, prod_imag], axis=1), ('col', 'limb'))  15.3 us
    all_to_all x1, waiting for transfers between devices, body(): lax.all_to_all(hint_block[:, None, :], 'row', split_axis=2, concat_axis=1...  13.3 us
  transfers between devices with their start and end apart: 2, of which 2 were waited for; matrix products, arithmetic and copies ran while one was open for 0% of the time, Pallas kernels for 0%

profile of v1, /device:TPU:0, one launch (start us, length us, event | category | flops | bytes accessed | tf_op | source)
XLA Modules:
  0.0 495.1 jit_solution(14232134233034930929)
XLA Ops:
  6.5 1.6 copy-done
  8.1 9.6 %fusion.28 = f32[512,2048]{1,0:T(8,128)} fusion(bf16[2048,2048]{1,0:T(8,128)(2,1)} %param.3, bf16[2048,1,512]{2,0,1:T(8,128)(2,1)S(1)} %copy-done), kind=kOutput, calls=%fused_computation.22 | convolution fusion | flops 4294967296 | bytes 14680064 | tf_op jit(solution)/shard_map/dot_general | solution.py:21
  17.8 79.7 %reduce-scatter.2.cloned.1.call-done = f32[128,2048]{1,0:T(8,128)} async-done(((f32[512,2048]{1,0:T(8,128)}), f32[128,2048]{1,0:T(8,128)}) %reduce-scatter.2.cloned.1.call-update) | async-done | bytes 1048592 | tf_op jit(solution)/shard_map/reduce_scatter | solution.py:20
  97.4 3.6 copy.9
  101.0 3.6 all-to-all-start
  104.6 0.2 fusion.34
  104.8 13.3 %all-to-all-done = f32[128,1,2048]{0,1,2:T(1,128)S(1)} async-done(((f32[128,1,2048]{0,1,2:T(1,128)}), f32[128,1,2048]{0,1,2:T(1,128)S(1)}, u32[]{:S(2)}, u32[]{:S(2)}) %all-to-all-start) | async-done | bytes 1048608 | tf_op jit(solution)/shard_map/all_to_all | solution.py:28
  118.1 1.0 copy-done.2
  119.1 1.6 copy.15
  120.7 3.9 convolution_negate_fusion
  124.6 4.7 add_bitcast_fusion
  129.4 0.9 pad_maximum_fusion
  130.3 0.7 copy.11
  131.0 26.6 %all_to_all.21 = f32[2,128,2,1024]{3,1,0,2:T(8,128)S(1)} all-to-all(f32[2,128,2,1024]{3,1,0,2:T(8,128)S(1)} %copy.11), channel_id=1, replica_groups=mesh['grp'=2,'col'=4,'row'=2,'limb'=2] {'row'}, dimensions={2} | all-to-all | bytes 4194304 | tf_op jit(solution)/shard_map/all_to_all | solution.py:46
  157.6 1.2 fusion.69
  158.8 2.5 copy.17
  161.3 77.7 %fusion.8 = f32[128,2048]{1,0:T(8,128)} fusion(f32[128,2048]{0,1:T(8,128)} %bitcast.52), kind=kOutput, calls=%fused_computation.11 | convolution fusion | flops 6501171200 | bytes 2097152 | tf_op jit(solution)/shard_map/dot_general | solution.py:9
  239.0 1.3 copy.16
  240.4 77.4 %fusion.10 = f32[128,2048]{1,0:T(8,128)S(1)} fusion(f32[128,2048]{0,1:T(8,128)} %bitcast.55), kind=kOutput, calls=%fused_computation.12 | convolution fusion | flops 6501171200 | bytes 2097152 | tf_op jit(solution)/shard_map/dot_general | solution.py:9
  317.8 76.7 %fusion.22 = f32[128,2048]{1,0:T(8,128)S(1)} fusion(f32[128,2048]{1,0:T(8,128)S(1)} %copy-done.5, f32[128,2048]{0,1:T(8,128)S(1)} %bitcast.56), kind=kOutput, calls=%fused_computation.17 | convolution fusion | flops 6501695488 | bytes 3145728 | tf_op jit(solution)/shard_map/dot_general | solution.py:9
  394.5 76.5 %fusion.25 = f32[128,2048]{1,0:T(8,128)S(1)} fusion(f32[128,2048]{1,0:T(8,128)S(1)} %fusion.10, f32[128,2048]{0,1:T(8,128)S(1)} %bitcast.53), kind=kOutput, calls=%fused_computation.18 | convolution fusion | flops 6501695488 | bytes 3145728 | tf_op jit(solution)/shard_map/dot_general | solution.py:9
  471.1 0.8 subtract_reduce_fusion
  472.0 15.3 %all-gather = f32[16,2,2048]{2,1,0:T(2,128)S(1)} all-gather(f32[2,2,2048]{2,1,0:T(2,128)S(1)} %pad_maximum_fusion.1), channel_id=2, replica_groups=mesh['grp'=2,'col'=4,'row'=2,'limb'=2] {'col','limb'}, dimensions={0}, use_global_device_ids=true | all-gather | bytes 294912 | tf_op jit(solution)/shard_map/all_gather | solution.py:63
  487.4 0.6 broadcast_multiply_fusion
  (18 shorter events, 0.2 us)
Async XLA Ops:
  6.5 1.6 copy-start
  6.5 90.9 %reduce-scatter.2.cloned.1.call-start = ((), (), s32[]{:S(2)}) async-start(), calls=%async_computation.3 | async-start | bytes 5242880 | tf_op jit(solution)/shard_map/reduce_scatter | solution.py:20
  101.0 17.1 %all-to-all-start = ((f32[128,1,2048]{0,1,2:T(1,128)}), f32[128,1,2048]{0,1,2:T(1,128)S(1)}, u32[]{:S(2)}, u32[]{:S(2)}) async-start(f32[128,1,2048]{0,1,2:T(1,128)} %copy.9), calls=%async_computation.1 | async-start | bytes 2097152 | tf_op jit(solution)/shard_map/all_to_all | solution.py:28
  118.1 1.0 copy-start.2
  240.4 77.4 %copy-start.4 = (f32[1,128,2,1024]{1,3,2,0:T(8,128)S(1)}, f32[1,128,2,1024]{1,3,2,0:T(8,128)}, u32[]{:S(2)}) copy-start(f32[1,128,2,1024]{1,3,2,0:T(8,128)} %copy.16) | copy-start | bytes 3145732
  240.4 77.4 %copy-start.5 = (f32[128,2048]{1,0:T(8,128)S(1)}, f32[128,2048]{1,0:T(8,128)}, u32[]{:S(2)}) copy-start(f32[128,2048]{1,0:T(8,128)} %fusion.8) | copy-start | bytes 3145732
  317.8 76.8 %copy-start.3 = (f32[1,128,2,1024]{1,3,2,0:T(8,128)S(1)}, f32[1,128,2,1024]{1,3,2,0:T(8,128)}, u32[]{:S(2)}) copy-start(f32[1,128,2,1024]{1,3,2,0:T(8,128)} %copy.17) | copy-start | bytes 3145732
  394.5 76.5 %copy-start.1 = (f32[2,2,1,128,2048]{4,3,2,1,0:T(8,128)S(1)}, f32[2,2,1,128,2048]{4,3,2,1,0:T(8,128)}, u32[]{:S(2)}) copy-start(f32[2,2,1,128,2048]{4,3,2,1,0:T(8,128)} %param.5) | copy-start | bytes 12582916
Sparse Core Ops, SparseCore 0:
  17.9 79.5 reduce-scatter.1
